TPU v7x, 32 devices: a whole 2x2x4 slice. The times are simulated.
32 devices in a mesh: tensor: 4 (over z), seq: 8 (over y, x, core).
Axes of the slice: x: 2, y: 2, z: 4, core: 2. Of those that a mesh axis runs over, the one named last changes fastest.
Arguments:
- teacher_q: bfloat16 [4096, 8192], P('seq', 'tensor'), may hold values from -24 to 24
- teacher_v: bfloat16 [4096, 8192], P('seq', 'tensor'), may hold values from -24 to 24
- student_q: bfloat16 [4096, 2048], P('seq'), may hold values from -24 to 24
- student_v: bfloat16 [4096, 2048], P('seq'), may hold values from -24 to 24
Outputs:
- grad_q: bfloat16 [4096, 2048], P('seq')
- grad_v: bfloat16 [4096, 2048], P('seq')
All inputs are finite; a program needn't handle non-finite values.
Results may differ from a plain program's by a relative error of at most 0.0095.
Values may be sent and summed in bfloat16 or wider, within the bound.
A program may use at most 128 MiB of HBM per device.

v0:
```python
import jax
import jax.numpy as jnp
from jax import lax
from jax.sharding import PartitionSpec as P

HEADS = 32
SEQS = 2


def from_partner(array, axis, distance):
    return lax.ppermute(array, axis, [(i, i ^ 1 << distance) for i in range(lax.axis_size(axis))])


def head_terms(teach_query, teach_key, stud_query, stud_key, teach_dim, stud_dim):
    teach_scores = jnp.dot(
        teach_query, teach_key.T, preferred_element_type=jnp.float32
    ) * teach_dim ** (-0.5)
    stud_scores = jnp.dot(
        stud_query, stud_key.T, preferred_element_type=jnp.float32
    ) * stud_dim ** (-0.5)
    teach_prob = jax.nn.softmax(teach_scores, axis=-1)
    stud_prob = jax.nn.softmax(stud_scores, axis=-1)
    coef = (256.0 * stud_dim ** (-0.5) * (stud_prob - teach_prob)).astype(jnp.bfloat16)
    query_grad = jnp.dot(coef, stud_key, preferred_element_type=jnp.float32)
    key_grad = jnp.einsum("qk,qd->kd", coef, stud_query, preferred_element_type=jnp.float32)
    return (query_grad, key_grad)


def relate(teach_own, teach_keys, stud_own, stud_keys, per_dev, teach_dim, stud_dim):
    tok_rows = teach_own.shape[0]
    teach_query = teach_own.reshape(tok_rows, per_dev, teach_dim).transpose(1, 0, 2)
    teach_key = teach_keys.reshape(-1, per_dev, teach_dim).transpose(1, 0, 2)
    stud_query = stud_own.reshape(tok_rows, per_dev, stud_dim).transpose(1, 0, 2)
    stud_key = stud_keys.reshape(-1, per_dev, stud_dim).transpose(1, 0, 2)

    def one_head(group):
        return head_terms(group[0], group[1], group[2], group[3], teach_dim, stud_dim)

    query_grad, key_grad = lax.map(one_head, (teach_query, teach_key, stud_query, stud_key))
    return (
        query_grad.transpose(1, 0, 2).reshape(tok_rows, per_dev * stud_dim),
        key_grad.transpose(1, 0, 2).reshape(-1, per_dev * stud_dim),
    )


def shards(teacher_q, teacher_v, student_q, student_v):
    n_tensor = lax.axis_size("tensor")
    n_seq = lax.axis_size("seq")
    per_dev = HEADS // n_tensor
    group_size = n_seq // SEQS
    level_count = group_size.bit_length() - 1
    seq_index = lax.axis_index("seq")
    member = seq_index % group_size
    teach_dim = teacher_q.shape[1] // per_dev
    stud_dim = student_q.shape[1] // HEADS
    own_width = per_dev * stud_dim
    offset = lax.axis_index("tensor") * own_width
    own_q = lax.dynamic_slice_in_dim(student_q, offset, own_width, 1)
    own_v = lax.dynamic_slice_in_dim(student_v, offset, own_width, 1)
    key_tq, key_tv, key_sq, key_sv = (teacher_q, teacher_v, own_q, own_v)
    for bit_num in range(level_count):
        partner = from_partner((key_tq, key_tv, key_sq, key_sv), "seq", bit_num)
        upper_half = member // 2**bit_num % 2 == 1
        joined = []
        for mine, theirs in zip((key_tq, key_tv, key_sq, key_sv), partner):
            joined.append(
                jnp.where(
                    upper_half,
                    jnp.concatenate([theirs, mine], 0),
                    jnp.concatenate([mine, theirs], 0),
                )
            )
        key_tq, key_tv, key_sq, key_sv = joined
    q_query, q_key = relate(teacher_q, key_tq, own_q, key_sq, per_dev, teach_dim, stud_dim)
    v_query, v_key = relate(teacher_v, key_tv, own_v, key_sv, per_dev, teach_dim, stud_dim)
    returned = jnp.concatenate([q_key, v_key], axis=1)
    for bit_num in reversed(range(level_count)):
        half_rows = returned.shape[0] // 2
        upper_half = member // 2**bit_num % 2 == 1
        low_part = returned[:half_rows]
        high_part = returned[half_rows:]
        kept = jnp.where(upper_half, high_part, low_part)
        outgoing = jnp.where(upper_half, low_part, high_part)
        returned = kept + from_partner(outgoing.astype(jnp.bfloat16), "seq", bit_num).astype(
            outgoing.dtype
        )
    head_q = (q_query + returned[:, :own_width]).astype(jnp.bfloat16)
    head_v = (v_query + returned[:, own_width:]).astype(jnp.bfloat16)
    full_q, full_v = (
        lax.all_gather(head_q, "tensor", axis=1, tiled=True),
        lax.all_gather(head_v, "tensor", axis=1, tiled=True),
    )
    return (full_q, full_v)


def solution(mesh):
    in_specs = (P("seq", "tensor"), P("seq", "tensor"), P("seq", None), P("seq", None))
    out_specs = (P("seq", None), P("seq", None))
    return jax.shard_map(shards, mesh=mesh, in_specs=in_specs, out_specs=out_specs, check_vma=False)
```

profile of v0, /device:TPU:0, one launch (start us, length us, event | category | flops | bytes accessed | tf_op | source)
XLA Modules:
  0.0 555.9 jit_solution(9372963571637865610)
XLA Ops:
  7.2 4.0 copy.11
  11.7 4.1 collective-permute-done.2
  15.9 6.6 %maximum_select_fusion.2 = bf16[1024,2048]{0,1:T(8,128)(2,1)} fusion(bf16[512,2048]{0,1:T(8,128)(2,1)} %copy.11, bf16[512,2048]{0,1:T(8,128)(2,1)} %collective-permute-done.2, pred[]{:T(512)S(6)} %eq.15), kind=kLoop, calls=%fused_computation.66 | loop fusion | flops 18874368 | bytes 8388609 | tf_op jit(solution)/shard_map/jit(_where)/select_n | solution.py:67
  22.5 2.9 collective-permute-start.3
  25.7 3.9 copy.20
  33.3 2.6 maximum_select_fusion.8
  43.0 96.5 %collective-permute-done.1 = bf16[1024,512]{0,1:T(8,128)(2,1)} collective-permute-done((bf16[1024,512]{0,1:T(8,128)(2,1)}, bf16[1024,512]{0,1:T(8,128)(2,1)}, u32[]{:S(2)}, u32[]{:S(2)}) %collective-permute-start.1) | collective-permute-done | bytes 1048608 | tf_op jit(solution)/shard_map/ppermute | solution.py:11
  139.5 3.7 fusion.47
  143.2 18.3 %collective-permute-done.5 = bf16[1024,512]{0,1:T(8,128)(2,1)} collective-permute-done((bf16[1024,512]{0,1:T(8,128)(2,1)}, bf16[1024,512]{0,1:T(8,128)(2,1)}, u32[]{:S(2)}, u32[]{:S(2)}) %collective-permute-start.5) | collective-permute-done | bytes 1048608 | tf_op jit(solution)/shard_map/ppermute | solution.py:11
  161.5 3.7 fusion.48
  165.1 4.9 maximum_select_fusion.4
  171.8 5.3 maximum_select_fusion.3
  177.1 5.0 maximum_select_fusion.5
  182.1 8.9 %fusion.44 = bf16[8,2048,256]{1,2,0:T(8,128)(2,1)} fusion(bf16[1024,8,256]{0,2,1:T(8,128)(2,1)S(1)} %maximum_select_fusion.3, bf16[1024,8,256]{0,2,1:T(8,128)(2,1)} %bitcast.19, pred[]{:T(512)S(6)} %eq.14), kind=kLoop, calls=%fused_computation.59 | loop fusion | flops 37748736 | bytes 16777216 | tf_op jit(solution)/shard_map/transpose | solution.py:32
  191.0 2.5 broadcast.48.clone.1
  194.7 90.5 %while.24 = (s32[]{:T(128)}, f32[8,512,64]{1,2,0:T(8,128)}, f32[8,2048,64]{1,2,0:T(8,128)}, bf16[8,512,64]{1,2,0:T(8,128)(2,1)S(1)}, bf16[8,2048,64]{1,2,0:T(8,1...) while((s32[]{:T(128)}, f32[8,512,64]{1,2,0:T(8,128)}, ...), condition=%wide.region_5.6_spmd, body=%wide.region_0.5_spmd.sunk | while | flops 959444992 | bytes 34103380 | solution.py:39
  196.4 2.1 multiply_reduce_fusion.9
  200.4 2.0 multiply_convert_fusion.4
  203.6 2.4 fusion.74
  207.8 2.1 multiply_reduce_fusion.9
  211.7 2.0 multiply_convert_fusion.4
  214.9 2.4 fusion.74
  219.1 2.1 multiply_reduce_fusion.9
  223.0 2.0 multiply_convert_fusion.4
  226.3 2.4 fusion.74
  230.4 2.1 multiply_reduce_fusion.9
  234.3 2.0 multiply_convert_fusion.4
  237.6 2.4 fusion.74
  241.7 2.1 multiply_reduce_fusion.9
  248.9 2.4 fusion.74
  253.0 2.1 multiply_reduce_fusion.9
  260.2 2.4 fusion.74
  264.3 2.1 multiply_reduce_fusion.9
  271.5 2.4 fusion.74
  275.6 2.1 multiply_reduce_fusion.9
  282.8 2.4 fusion.74
  285.2 11.2 %fusion.45 = bf16[8,2048,256]{1,2,0:T(8,128)(2,1)} fusion(bf16[1024,8,256]{0,2,1:T(8,128)(2,1)} %maximum_select_fusion.5, bf16[1024,8,256]{0,2,1:T(8,128)(2,1)} %bitcast.33, pred[]{:T(512)S(6)} %eq.14), kind=kLoop, calls=%fused_computation.61 | loop fusion | flops 37748736 | bytes 16777216 | tf_op jit(solution)/shard_map/transpose | solution.py:32
  296.4 2.5 broadcast.48.clone
  300.0 90.5 %while.25 = (s32[]{:T(128)}, f32[8,512,64]{1,2,0:T(8,128)}, f32[8,2048,64]{1,2,0:T(8,128)}, bf16[8,512,64]{1,2,0:T(8,128)(2,1)S(1)}, bf16[8,2048,64]{1,2,0:T(8,1...) while((s32[]{:T(128)}, f32[8,512,64]{1,2,0:T(8,128)}, ...), condition=%wide.region_11.12_spmd, body=%wide.region_6.11_spmd.sunk | while | flops 959444992 | bytes 34103380 | solution.py:39
  301.8 2.1 multiply_reduce_fusion.11
  309.0 2.4 fusion.81
  313.1 2.1 multiply_reduce_fusion.11
  320.3 2.4 fusion.81
  324.5 2.1 multiply_reduce_fusion.11
  331.6 2.4 fusion.81
  335.8 2.1 multiply_reduce_fusion.11
  342.9 2.4 fusion.81
  347.1 2.1 multiply_reduce_fusion.11
  354.2 2.4 fusion.81
  358.4 2.1 multiply_reduce_fusion.11
  365.5 2.4 fusion.81
  369.7 2.1 multiply_reduce_fusion.11
  376.8 2.4 fusion.81
  381.0 2.1 multiply_reduce_fusion.11
  388.1 2.4 fusion.81
  390.5 4.1 select_convert_fusion
  394.9 46.3 %collective-permute-done.8 = bf16[1024,1024]{0,1:T(8,128)(2,1)S(1)} collective-permute-done((bf16[1024,1024]{0,1:T(8,128)(2,1)S(1)}, bf16[1024,1024]{0,1:T(8,128)(2,1)S(1)}, u32[]{:S(2)}, u32[]{:S(2)}) %collective-permute-start.8) | collective-permute-done | bytes 2097184 | tf_op jit(solution)/shard_map/ppermute | solution.py:11
  441.2 4.2 convert_add_fusion
  445.7 2.6 collective-permute-done.9
  449.0 2.9 fusion.49
  452.7 45.6 %all-gather.3.cloned.1.call-done = bf16[512,2048]{0,1:T(8,128)(2,1)} async-done(((bf16[512,512]{0,1:T(8,128)(2,1)}), bf16[512,2048]{0,1:T(8,128)(2,1)}) %all-gather.3.cloned.1.call-update) | async-done | bytes 2097168 | tf_op jit(solution)/shard_map/all_gather | solution.py:90
  498.3 3.9 copy.28
  502.2 42.9 %all-gather.5.cloned.1.call-done = bf16[512,2048]{0,1:T(8,128)(2,1)} async-done(((bf16[512,512]{0,1:T(8,128)(2,1)}), bf16[512,2048]{0,1:T(8,128)(2,1)}) %all-gather.5.cloned.1.call-update) | async-done | bytes 2097168 | tf_op jit(solution)/shard_map/all_gather | solution.py:91
  545.1 3.9 copy.29
  (95 shorter events, 118.6 us)
Async XLA Ops:
  7.2 18.2 %copy-start = (bf16[512,2048]{1,0:T(8,128)(2,1)S(1)}, bf16[512,2048]{1,0:T(8,128)(2,1)}, u32[]{:S(2)}) copy-start(bf16[512,2048]{1,0:T(8,128)(2,1)} %param.10) | copy-start | bytes 6291460
  7.2 491.1 %all-gather.3.cloned.1.call-start = ((), (), s32[]{:S(2)}) async-start(), calls=%async_computation | async-start | bytes 2621440 | tf_op jit(solution)/shard_map/all_gather | solution.py:90
  11.3 4.6 collective-permute-start.2
  22.5 159.6 %collective-permute-start.3 = (bf16[1024,2048]{0,1:T(8,128)(2,1)}, bf16[1024,2048]{0,1:T(8,128)(2,1)}, u32[]{:S(2)}, u32[]{:S(2)}) collective-permute-start(bf16[1024,2048]{0,1:T(8,128)(2,1)} %maximum_select_fusion.2), channel_id=1, source_target_pairs={{0,2},{1,3},{2,0},{3,1},{4,6},{5,7},{6,4},{7,5},{8,10},{9,11},{10,... | collective-permute-start | bytes 12582920 | tf_op jit(solution)/shard_map/ppermute | solution.py:11
  25.6 7.7 %collective-permute-start = (bf16[512,512]{0,1:T(8,128)(2,1)S(1)}, bf16[512,512]{0,1:T(8,128)(2,1)}, u32[]{:S(2)}, u32[]{:S(2)}) collective-permute-start(bf16[512,512]{0,1:T(8,128)(2,1)S(1)} %copy.38), channel_id=1, source_target_pairs={{0,1},{1,0},{2,3},{3,2},{4,5},{5,4},{6,7},{7,6},{8,9},{9,8},{10,11... | collective-permute-start | bytes 1572872 | tf_op jit(solution)/shard_map/ppermute | solution.py:11
  29.6 135.5 %collective-permute-start.6 = (bf16[512,2048]{0,1:T(8,128)(2,1)}, bf16[512,2048]{0,1:T(8,128)(2,1)S(1)}, u32[]{:S(2)}, u32[]{:S(2)}) collective-permute-start(bf16[512,2048]{0,1:T(8,128)(2,1)} %copy.20), channel_id=1, source_target_pairs={{0,1},{1,0},{2,3},{3,2},{4,5},{5,4},{6,7},{7,6},{8,9},{9,8},{10,11... | collective-permute-start | bytes 6291464 | tf_op jit(solution)/shard_map/ppermute | solution.py:11
  33.2 2.8 collective-permute-start.4
  35.9 103.6 %collective-permute-start.1 = (bf16[1024,512]{0,1:T(8,128)(2,1)}, bf16[1024,512]{0,1:T(8,128)(2,1)}, u32[]{:S(2)}, u32[]{:S(2)}) collective-permute-start(bf16[1024,512]{0,1:T(8,128)(2,1)} %maximum_select_fusion.8), channel_id=1, source_target_pairs={{0,2},{1,3},{2,0},{3,1},{4,6},{5,7},{6,4},{7,5},{8,10},{9,11},{10,... | collective-permute-start | bytes 3145736 | tf_op jit(solution)/shard_map/ppermute | solution.py:11
  36.0 0.8 copy-start.2
  38.1 123.4 %collective-permute-start.5 = (bf16[1024,512]{0,1:T(8,128)(2,1)}, bf16[1024,512]{0,1:T(8,128)(2,1)}, u32[]{:S(2)}, u32[]{:S(2)}) collective-permute-start(bf16[1024,512]{0,1:T(8,128)(2,1)} %maximum_select_fusion.10), channel_id=1, source_target_pairs={{0,2},{1,3},{2,0},{3,1},{4,6},{5,7},{6,4},{7,5},{8,10},{9,11},{10,... | collective-permute-start | bytes 3145736 | tf_op jit(solution)/shard_map/ppermute | solution.py:11
  170.1 115.1 %collective-permute-start.7 = (bf16[1024,2048]{0,1:T(8,128)(2,1)}, bf16[1024,2048]{0,1:T(8,128)(2,1)}, u32[]{:S(2)}, u32[]{:S(2)}) collective-permute-start(bf16[1024,2048]{0,1:T(8,128)(2,1)} %maximum_select_fusion.4), channel_id=1, source_target_pairs={{0,2},{1,3},{2,0},{3,1},{4,6},{5,7},{6,4},{7,5},{8,10},{9,11},{10,... | collective-permute-start | bytes 12582920 | tf_op jit(solution)/shard_map/ppermute | solution.py:11
  394.6 46.6 %collective-permute-start.8 = (bf16[1024,1024]{0,1:T(8,128)(2,1)S(1)}, bf16[1024,1024]{0,1:T(8,128)(2,1)S(1)}, u32[]{:S(2)}, u32[]{:S(2)}) collective-permute-start(bf16[1024,1024]{0,1:T(8,128)(2,1)S(1)} %select_convert_fusion), channel_id=1, source_target_pairs={{0,2},{1,3},{2,0},{3,1},{4,6},{5,7},{6,4},{7,5},{8,10},{9,11},{10,... | collective-permute-start | bytes 6291464 | tf_op jit(solution)/shard_map/ppermute | solution.py:11
  445.6 2.7 collective-permute-start.9
  451.9 93.2 %all-gather.5.cloned.1.call-start = ((), (), s32[]{:S(2)}) async-start(), calls=%async_computation.1 | async-start | bytes 2621440 | tf_op jit(solution)/shard_map/all_gather | solution.py:91
  452.7 96.4 %copy-start.1 = (bf16[512,2048]{1,0:T(8,128)(2,1)S(1)}, bf16[512,2048]{1,0:T(8,128)(2,1)}, u32[]{:S(2)}) copy-start(bf16[512,2048]{1,0:T(8,128)(2,1)} %param.10) | copy-start | bytes 6291460
Sparse Core Ops, SparseCore 0:
  452.0 46.2 all-gather.2
  500.5 44.6 all-gather.4
where the time goes:
time: 558 us; the launch traced here: 556 us
  waiting for transfers between devices  257 us (46%)
  other arithmetic  128 us (23%)
  matrix products  121 us (22%)
  local copies, waits for them, and re-layouts  27.2 us (5%)
  between operations  14.2 us (3%)
  starting transfers between devices  8.22 us (1%)
    ppermute x10, waiting for transfers between devices, from_partner(): lax.ppermute(array, axis, [(i, i ^ 1 << distance) for i in range(lax.axis...  168 us
    all_gather x1, waiting for transfers between devices, shards(): lax.all_gather(head_q, 'tensor', axis=1, tiled=True)  45.6 us
    all_gather x1, waiting for transfers between devices, shards(): lax.all_gather(head_v, 'tensor', axis=1, tiled=True)  42.9 us
    dot_general x16, matrix products, head_terms(): query_grad = jnp.dot(coef, stud_key, preferred_element_type=jnp.float32)  37.8 us
    dot_general x16, matrix products, head_terms(): jnp.dot(teach_query, teach_key.T, preferred_element_type=jnp.float32)  34.1 us
    convert_element_type x16, other arithmetic, head_terms(): (256.0 * stud_dim ** (-0.5) * (stud_prob - teach_prob)).astype(jnp.bfloat16)  31.4 us
    select_n x8, other arithmetic, shards(): jnp.where(upper_half, jnp.concatenate([theirs, mine], 0), jnp.concatenate...  28.7 us
    reduce_sum x16, other arithmetic, head_terms(): stud_prob = jax.nn.softmax(stud_scores, axis=-1)  28.5 us
  transfers between devices with their start and end apart: 12, of which 7 were waited for; matrix products, arithmetic and copies ran while one was open for 26% of the time, Pallas kernels for 0%

commit v1 on v0

--- a/solution.py
+++ b/solution.py
@@ -1,10 +1,100 @@
+import functools
+import math
+
 import jax
 import jax.numpy as jnp
 from jax import lax
+from jax.experimental import pallas as pl
+from jax.experimental.pallas import tpu as pltpu
 from jax.sharding import PartitionSpec as P
 
 HEADS = 32
 SEQS = 2
+BLOCK = 256
+LOG2E = math.log2(math.e)
+
+
+def softmax_terms(scores, scale):
+    scaled = scores * (scale * LOG2E)
+    shifted = jnp.exp2(scaled - jnp.max(scaled, axis=0, keepdims=True))
+    return shifted, jnp.sum(shifted, axis=0, keepdims=True)
+
+
+def pair_block(teach, stud, stud_t, grad, start, tdh, sdh):
+    rows = pl.ds(start, BLOCK)
+    stud_own = stud[rows, :]
+    lane = lax.broadcasted_iota(jnp.int32, stud_own.shape, 1)
+    key_side = None
+    query_side = []
+    for head in range(2):
+        columns = slice(head * tdh, (head + 1) * tdh)
+        masked = jnp.where(lane // sdh == head, stud_own, jnp.zeros_like(stud_own))
+        dims = (((1,), (1,)), ((), ()))
+        teach_scores = lax.dot_general(teach[:, columns], teach[rows, columns], dims, preferred_element_type=jnp.float32)
+        stud_scores = lax.dot_general(stud[...], masked, dims, preferred_element_type=jnp.float32)
+        teach_exp, teach_sum = softmax_terms(teach_scores, tdh**-0.5)
+        stud_exp, stud_sum = softmax_terms(stud_scores, sdh**-0.5)
+        factor = 256.0 * sdh**-0.5
+        coef = (stud_exp * (factor / stud_sum) - teach_exp * (factor / teach_sum)).astype(jnp.bfloat16)
+        part = jnp.dot(coef, masked, preferred_element_type=jnp.float32)
+        key_side = part if key_side is None else key_side + part
+        query_side.append(
+            jnp.dot(stud_t[head * sdh : (head + 1) * sdh, :], coef, preferred_element_type=jnp.float32)
+        )
+    grad[...] += key_side
+    grad[rows, :] += jnp.concatenate(query_side, axis=0).T
+
+
+def pair_kernel(tdh, sdh, teach, stud, out, stud_t, grad):
+    length = teach.shape[0]
+    stud_t[...] = stud[...].T
+    grad[...] = jnp.zeros_like(grad)
+
+    @pl.loop(0, length // BLOCK)
+    def _(block):
+        pair_block(teach, stud, stud_t, grad, pl.multiple_of(block * BLOCK, BLOCK), tdh, sdh)
+
+    out[...] = grad[...].astype(out.dtype)
+
+
+def pair_grad(teach, stud, tdh, sdh):
+    length = teach.shape[0]
+    return pl.pallas_call(
+        functools.partial(pair_kernel, tdh, sdh),
+        out_shape=jax.ShapeDtypeStruct((length, 2 * sdh), jnp.bfloat16),
+        in_specs=[pl.BlockSpec(memory_space=pltpu.VMEM)] * 2,
+        out_specs=pl.BlockSpec(memory_space=pltpu.VMEM),
+        scratch_shapes=[
+            pltpu.VMEM((2 * sdh, length), jnp.bfloat16),
+            pltpu.VMEM((length, 2 * sdh), jnp.float32),
+        ],
+        compiler_params=pltpu.CompilerParams(vmem_limit_bytes=56 * 2**20),
+    )(teach, stud)
+
+
+def shards_pairs(teacher_q, teacher_v, student_q, student_v):
+    n_tensor = lax.axis_size("tensor")
+    n_seq = lax.axis_size("seq")
+    group_size = n_seq // SEQS
+    groups = [[s * group_size + m for m in range(group_size)] for s in range(SEQS)]
+    per_dev = HEADS // n_tensor
+    tdh = teacher_q.shape[1] // per_dev
+    sdh = student_q.shape[1] // HEADS
+    own_width = per_dev * sdh
+    offset = lax.axis_index("tensor") * own_width
+
+    def exchange(array, split_axis, concat_axis):
+        return lax.all_to_all(
+            array, "seq", split_axis, concat_axis, tiled=True, axis_index_groups=groups
+        )
+
+    def relation(teacher, student):
+        teach = exchange(teacher, 1, 0)
+        stud = exchange(lax.dynamic_slice_in_dim(student, offset, own_width, 1), 1, 0)
+        grad = pair_grad(teach, stud, tdh, sdh)
+        return lax.all_gather(exchange(grad, 0, 1), "tensor", axis=1, tiled=True)
+
+    return (relation(teacher_q, student_q), relation(teacher_v, student_v))
 
 
 def from_partner(array, axis, distance):
@@ -94,6 +184,9 @@
 
 
 def solution(mesh):
+    per_dev = HEADS // mesh.shape["tensor"]
+    group_size = mesh.shape["seq"] // SEQS
+    body = shards_pairs if per_dev == 2 * group_size else shards
     in_specs = (P("seq", "tensor"), P("seq", "tensor"), P("seq", None), P("seq", None))
     out_specs = (P("seq", None), P("seq", None))
-    return jax.shard_map(shards, mesh=mesh, in_specs=in_specs, out_specs=out_specs, check_vma=False)
+    return jax.shard_map(body, mesh=mesh, in_specs=in_specs, out_specs=out_specs, check_vma=False)

time: 558 us -> 258 us (0.46)
  waiting for transfers between devices: 257 us -> 111 us
  other arithmetic: 128 us -> 0 us
  matrix products: 121 us -> 0 us
  Pallas kernels: 0 us -> 75.4 us
  blocking collectives: 0 us -> 24.6 us
  local copies, waits for them, and re-layouts: 27.2 us -> 17.5 us
  starting transfers between devices: 8.22 us -> 15 us
    ppermute x10 -> x0, waiting for transfers between devices: 168 us -> none  [from_partner(): lax.ppermute(array, axis, [(i, i ^ 1 << distance) for i in range(lax.axis...]
    dot_general x64 -> x0, matrix products: 121 us -> none  [the longest x16 37.8 us: head_terms(): query_grad = jnp.dot(coef, stud_key, preferred_element_type=jnp.float32)]
    pallas_call x0 -> x2, Pallas kernels: none -> 75.4 us  [pair_grad(): pl.pallas_call(functools.partial(pair_kernel, tdh, sdh), out_shape=jax.Sh...]
    all_to_all x0 -> x4, waiting for transfers between devices: none -> 63.8 us  [exchange(): lax.all_to_all(array, 'seq', split_axis, concat_axis, tiled=True, axis_in...]
    all_gather x2, waiting for transfers between devices: 88.6 us -> 47.1 us  [relation(): return lax.all_gather(exchange(grad, 0, 1), 'tensor', axis=1, tiled=True)]
    convert_element_type x19 -> x0, other arithmetic: 38.5 us -> none  [the longest x16 31.4 us: head_terms(): (256.0 * stud_dim ** (-0.5) * (stud_prob - teach_prob)).astype(jnp.bfloat16)]
    select_n x8 -> x0, other arithmetic: 28.7 us -> none  [shards(): jnp.where(upper_half, jnp.concatenate([theirs, mine], 0), jnp.concatenate...]
    reduce_sum x16 -> x0, other arithmetic: 28.5 us -> none  [head_terms(): stud_prob = jax.nn.softmax(stud_scores, axis=-1)]
  transfers between devices with their start and end apart: 12 -> 6, of which waited for: 7 -> 5; matrix products, arithmetic and copies ran while one was open for 26% -> 3% of each run, Pallas kernels for 0% -> 15%
where the time goes in v1:
time: 258 us; the launch traced here: 257 us
  waiting for transfers between devices  111 us (43%)
  Pallas kernels  75.4 us (29%)
  blocking collectives  24.6 us (10%)
  local copies, waits for them, and re-layouts  17.5 us (7%)
  starting transfers between devices  15 us (6%)
  between operations  14.1 us (5%)
    pallas_call x2, Pallas kernels, pair_grad(): pl.pallas_call(functools.partial(pair_kernel, tdh, sdh), out_shape=jax.Sh...  75.4 us
    all_to_all x4, waiting for transfers between devices, exchange(): lax.all_to_all(array, 'seq', split_axis, concat_axis, tiled=True, axis_in...  63.8 us
    all_gather x2, waiting for transfers between devices, relation(): return lax.all_gather(exchange(grad, 0, 1), 'tensor', axis=1, tiled=True)  47.1 us
    all_to_all x2, blocking collectives, exchange(): lax.all_to_all(array, 'seq', split_axis, concat_axis, tiled=True, axis_in...  24.6 us
    all_to_all x4, starting transfers between devices, exchange(): lax.all_to_all(array, 'seq', split_axis, concat_axis, tiled=True, axis_in...  14.9 us
    unnamed x14, local copies, waits for them, and re-layouts  9.29 us
    all_to_all x6, local copies, waits for them, and re-layouts, exchange(): lax.all_to_all(array, 'seq', split_axis, concat_axis, tiled=True, axis_in...  6.74 us
  transfers between devices with their start and end apart: 6, of which 5 were waited for; matrix products, arithmetic and copies ran while one was open for 3% of the time, Pallas kernels for 15%

profile of v1, /device:TPU:0, one launch (start us, length us, event | category | flops | bytes accessed | tf_op | source)
XLA Modules:
  0.0 257.4 jit_solution(15157076872066447321)
XLA Ops:
  7.2 0.0 copy-start.2
  7.2 1.4 constant_dynamic-slice_fusion
  8.6 1.0 copy.18
  9.6 4.2 %all-to-all-start.1 = ((bf16[512,4,128]{0,2,1:T(8,128)(2,1)}), bf16[512,4,128]{0,2,1:T(8,128)(2,1)S(1)}, u32[]{:S(2)}, u32[]{:S(2)}) async-start(bf16[512,4,128]{0,2,1:T(8,128)(2,1)} %bitcast.40), calls=%async_computation.1 | async-start | bytes 1048576 | tf_op jit(solution)/shard_map/all_to_all | solution.py:87
  13.8 0.0 copy-done.2
  13.8 1.5 copy.29
  15.3 7.3 %all-to-all-done.1 = bf16[512,4,128]{0,2,1:T(8,128)(2,1)S(1)} async-done(((bf16[512,4,128]{0,2,1:T(8,128)(2,1)}), bf16[512,4,128]{0,2,1:T(8,128)(2,1)S(1)}, u32[]{:S(2)}, u32[]{:S(2)}) %all-to-all-start.1) | async-done | bytes 524320 | tf_op jit(solution)/shard_map/all_to_all | solution.py:87
  22.7 3.6 %all-to-all-start = ((bf16[512,4,512]{2,0,1:T(8,128)(2,1)}), bf16[512,4,512]{2,0,1:T(8,128)(2,1)S(1)}, u32[]{:S(2)}, u32[]{:S(2)}) async-start(bf16[512,4,512]{2,0,1:T(8,128)(2,1)} %bitcast.33), calls=%async_computation | async-start | bytes 4194304 | tf_op jit(solution)/shard_map/all_to_all | solution.py:87
  26.3 0.0 all-gather.3.cloned.1.call-start
  26.3 1.0 copy.12
  27.3 24.6 %all-to-all-done = bf16[512,4,512]{2,0,1:T(8,128)(2,1)S(1)} async-done(((bf16[512,4,512]{2,0,1:T(8,128)(2,1)}), bf16[512,4,512]{2,0,1:T(8,128)(2,1)S(1)}, u32[]{:S(2)}, u32[]{:S(2)}) %all-to-all-start) | async-done | bytes 2097184 | tf_op jit(solution)/shard_map/all_to_all | solution.py:87
  51.9 0.0 copy-start
  52.0 1.3 copy-done
  53.3 37.7 %shard_map.59 = bf16[2048,128]{1,0:T(8,128)(2,1)} custom-call(bf16[2048,512]{1,0:T(8,128)(2,1)} %bitcast.34, bf16[2048,128]{1,0:T(8,128)(2,1)} %bitcast.41), custom_call_target="tpu_custom_call" | custom-call | tf_op jit(solution)/shard_map/pallas_call | solution.py:62
  90.9 12.3 %all_to_all.114 = bf16[4,512,128]{2,1,0:T(8,128)(2,1)S(1)} all-to-all(bf16[4,512,128]{2,1,0:T(8,128)(2,1)} %bitcast.43), channel_id=1, replica_groups={{0,1,2,3},{4,5,6,7},{8,9,10,11},{12,13,14,15},{16,17,18,19},{20,21,22,2..., dimensions={0} | all-to-all | bytes 1048576 | tf_op jit(solution)/shard_map/all_to_all | solution.py:87
  103.2 0.0 copy-start.3
  103.2 0.9 copy_bitcast_fusion.3
  104.1 0.0 all-gather.3.cloned.1.call-update
  104.1 1.0 copy.19
  105.1 3.5 %all-to-all-start.4 = ((bf16[512,4,128]{0,2,1:T(8,128)(2,1)}), bf16[512,4,128]{0,2,1:T(8,128)(2,1)S(1)}, u32[]{:S(2)}, u32[]{:S(2)}) async-start(bf16[512,4,128]{0,2,1:T(8,128)(2,1)} %bitcast.9), calls=%async_computation.4 | async-start | bytes 1048576 | tf_op jit(solution)/shard_map/all_to_all | solution.py:87
  108.6 0.0 copy-done.3
  108.6 1.5 copy.28
  110.1 7.3 %all-to-all-done.4 = bf16[512,4,128]{0,2,1:T(8,128)(2,1)S(1)} async-done(((bf16[512,4,128]{0,2,1:T(8,128)(2,1)}), bf16[512,4,128]{0,2,1:T(8,128)(2,1)S(1)}, u32[]{:S(2)}, u32[]{:S(2)}) %all-to-all-start.4) | async-done | bytes 524320 | tf_op jit(solution)/shard_map/all_to_all | solution.py:87
  117.4 3.6 %all-to-all-start.3 = ((bf16[512,4,512]{2,0,1:T(8,128)(2,1)}), bf16[512,4,512]{2,0,1:T(8,128)(2,1)S(1)}, u32[]{:S(2)}, u32[]{:S(2)}) async-start(bf16[512,4,512]{2,0,1:T(8,128)(2,1)} %bitcast.32), calls=%async_computation.3 | async-start | bytes 4194304 | tf_op jit(solution)/shard_map/all_to_all | solution.py:87
  121.0 0.0 all-gather.5.cloned.1.call-start
  121.1 1.0 copy.16
  122.1 24.6 %all-to-all-done.3 = bf16[512,4,512]{2,0,1:T(8,128)(2,1)S(1)} async-done(((bf16[512,4,512]{2,0,1:T(8,128)(2,1)}), bf16[512,4,512]{2,0,1:T(8,128)(2,1)S(1)}, u32[]{:S(2)}, u32[]{:S(2)}) %all-to-all-start.3) | async-done | bytes 2097184 | tf_op jit(solution)/shard_map/all_to_all | solution.py:87
  146.7 0.0 copy-start.1
  146.7 1.3 copy-done.1
  148.0 37.7 %shard_map.60 = bf16[2048,128]{1,0:T(8,128)(2,1)} custom-call(bf16[2048,512]{1,0:T(8,128)(2,1)} %bitcast.35, bf16[2048,128]{1,0:T(8,128)(2,1)} %bitcast.42), custom_call_target="tpu_custom_call" | custom-call | tf_op jit(solution)/shard_map/pallas_call | solution.py:62
  185.7 12.3 %all_to_all.115 = bf16[4,512,128]{2,1,0:T(8,128)(2,1)S(1)} all-to-all(bf16[4,512,128]{2,1,0:T(8,128)(2,1)} %bitcast.44), channel_id=1, replica_groups={{0,1,2,3},{4,5,6,7},{8,9,10,11},{12,13,14,15},{16,17,18,19},{20,21,22,2..., dimensions={0} | all-to-all | bytes 1048576 | tf_op jit(solution)/shard_map/all_to_all | solution.py:87
  198.0 0.9 copy_bitcast_fusion.2
  198.8 0.0 all-gather.5.cloned.1.call-update
  198.8 0.0 all-gather.3.cloned.1.call-done
  198.9 47.1 %all-gather.5.cloned.1.call-done = bf16[512,2048]{1,0:T(8,128)(2,1)} async-done(((bf16[512,512]{1,0:T(8,128)(2,1)}), bf16[512,2048]{1,0:T(8,128)(2,1)}) %all-gather.5.cloned.1.call-update) | async-done | bytes 2097168 | tf_op jit(solution)/shard_map/all_gather | solution.py:95
  245.9 0.0 copy-start.4
  246.0 3.3 %copy.32 = bf16[512,2048]{1,0:T(8,128)(2,1)} copy(bf16[512,2048]{1,0:T(8,128)(2,1)} %all-gather.3.cloned.1.call-done) | data formatting | bytes 4194304
  249.3 0.0 copy-done.4
  249.3 1.3 copy.33
Async XLA Ops:
  7.2 6.7 %copy-start.2 = (bf16[512,2048]{1,0:T(8,128)(2,1)S(1)}, bf16[512,2048]{1,0:T(8,128)(2,1)}, u32[]{:S(2)}) copy-start(bf16[512,2048]{1,0:T(8,128)(2,1)} %param.4) | copy-start | bytes 6291460
  9.6 13.1 %all-to-all-start.1 = ((bf16[512,4,128]{0,2,1:T(8,128)(2,1)}), bf16[512,4,128]{0,2,1:T(8,128)(2,1)S(1)}, u32[]{:S(2)}, u32[]{:S(2)}) async-start(bf16[512,4,128]{0,2,1:T(8,128)(2,1)} %bitcast.40), calls=%async_computation.1 | async-start | bytes 1048576 | tf_op jit(solution)/shard_map/all_to_all | solution.py:87
  22.7 29.3 %all-to-all-start = ((bf16[512,4,512]{2,0,1:T(8,128)(2,1)}), bf16[512,4,512]{2,0,1:T(8,128)(2,1)S(1)}, u32[]{:S(2)}, u32[]{:S(2)}) async-start(bf16[512,4,512]{2,0,1:T(8,128)(2,1)} %bitcast.33), calls=%async_computation | async-start | bytes 4194304 | tf_op jit(solution)/shard_map/all_to_all | solution.py:87
  26.3 172.6 %all-gather.3.cloned.1.call-start = ((), (), s32[]{:S(2)}) async-start(), calls=%async_computation.6 | async-start | bytes 2621440 | tf_op jit(solution)/shard_map/all_gather | solution.py:95
  51.9 1.3 copy-start
  103.2 5.4 %copy-start.3 = (bf16[512,2048]{1,0:T(8,128)(2,1)S(1)}, bf16[512,2048]{1,0:T(8,128)(2,1)}, u32[]{:S(2)}) copy-start(bf16[512,2048]{1,0:T(8,128)(2,1)} %param.5) | copy-start | bytes 6291460
  105.1 12.3 %all-to-all-start.4 = ((bf16[512,4,128]{0,2,1:T(8,128)(2,1)}), bf16[512,4,128]{0,2,1:T(8,128)(2,1)S(1)}, u32[]{:S(2)}, u32[]{:S(2)}) async-start(bf16[512,4,128]{0,2,1:T(8,128)(2,1)} %bitcast.9), calls=%async_computation.4 | async-start | bytes 1048576 | tf_op jit(solution)/shard_map/all_to_all | solution.py:87
  117.4 29.3 %all-to-all-start.3 = ((bf16[512,4,512]{2,0,1:T(8,128)(2,1)}), bf16[512,4,512]{2,0,1:T(8,128)(2,1)S(1)}, u32[]{:S(2)}, u32[]{:S(2)}) async-start(bf16[512,4,512]{2,0,1:T(8,128)(2,1)} %bitcast.32), calls=%async_computation.3 | async-start | bytes 4194304 | tf_op jit(solution)/shard_map/all_to_all | solution.py:87
  121.0 124.9 %all-gather.5.cloned.1.call-start = ((), (), s32[]{:S(2)}) async-start(), calls=%async_computation.7 | async-start | bytes 2621440 | tf_op jit(solution)/shard_map/all_gather | solution.py:95
  146.7 1.3 copy-start.1
  245.9 3.3 %copy-start.4 = (bf16[512,2048]{1,0:T(8,128)(2,1)S(1)}, bf16[512,2048]{1,0:T(8,128)(2,1)}, u32[]{:S(2)}) copy-start(bf16[512,2048]{1,0:T(8,128)(2,1)} %all-gather.5.cloned.1.call-done) | copy-start | bytes 6291460
Sparse Core Ops, SparseCore 0:
  104.2 46.9 all-gather.2
  199.0 46.9 all-gather.4

commit v2 on v0

--- a/solution.py
+++ b/solution.py
@@ -1,10 +1,255 @@
+import functools
+import math
+
 import jax
 import jax.numpy as jnp
 from jax import lax
+from jax.experimental import pallas as pl
+from jax.experimental.pallas import tpu as pltpu
 from jax.sharding import PartitionSpec as P
 
 HEADS = 32
 SEQS = 2
+BLOCK = 256
+FORWARD_AFTER = 2
+LOG2E = math.log2(math.e)
+
+
+def softmax_terms(scores, scale):
+    scaled = scores * (scale * LOG2E)
+    shifted = jnp.exp2(scaled - jnp.max(scaled, axis=0, keepdims=True))
+    return shifted, jnp.sum(shifted, axis=0, keepdims=True)
+
+
+def head_block(teach, stud, stud_t, grad, head, start, tdh, sdh):
+    rows = pl.ds(start, BLOCK)
+    columns = slice(head * tdh, (head + 1) * tdh)
+    dims = (((1,), (1,)), ((), ()))
+    stud_own = stud[rows, :]
+    lane = lax.broadcasted_iota(jnp.int32, stud_own.shape, 1)
+    masked = jnp.where(lane // sdh == head, stud_own, jnp.zeros_like(stud_own))
+    teach_scores = lax.dot_general(
+        teach[:, columns], teach[rows, columns], dims, preferred_element_type=jnp.float32
+    )
+    stud_scores = lax.dot_general(stud[...], masked, dims, preferred_element_type=jnp.float32)
+    teach_exp, teach_sum = softmax_terms(teach_scores, tdh**-0.5)
+    stud_exp, stud_sum = softmax_terms(stud_scores, sdh**-0.5)
+    factor = 256.0 * sdh**-0.5
+    coef = (stud_exp * (factor / stud_sum) - teach_exp * (factor / teach_sum)).astype(jnp.bfloat16)
+    grad[...] += jnp.dot(coef, masked, preferred_element_type=jnp.float32)
+    query_side = jnp.dot(stud_t[...], coef, preferred_element_type=jnp.float32)
+    sub = lax.broadcasted_iota(jnp.int32, query_side.shape, 0)
+    query_side = jnp.where(sub // sdh == head, query_side, 0.0)
+    grad[rows, :] += query_side.T
+
+
+def head_pass(teach, stud, stud_t, grad, head, first, last, tdh, sdh):
+    @pl.loop(first, last)
+    def _(block):
+        head_block(teach, stud, stud_t, grad, head, pl.multiple_of(block * BLOCK, BLOCK), tdh, sdh)
+
+
+def fused_kernel(
+    n_tensor, group_size, tdh, sdh,
+    teacher_q, teacher_v, student_q, student_v, out_q, out_v,
+    teach, stud, stud_t, grad, result,
+    teach_send, teach_recv, teach_local, stud_send, stud_recv, stud_local,
+    out_send, out_recv, out_local, fwd_send, fwd_recv,
+):
+    tensor = lax.axis_index("tensor")
+    seq = lax.axis_index("seq")
+    member = lax.rem(seq, group_size)
+    base = seq - member
+    teachers, students, outs = (teacher_q, teacher_v), (student_q, student_v), (out_q, out_v)
+    tok = teacher_q.shape[0]
+    length = tok * group_size
+    pair = 2 * sdh
+    blocks = length // BLOCK
+
+    def to(step):
+        return lax.rem(member + step, group_size)
+
+    def source(step):
+        return lax.rem(member + group_size - step, group_size)
+
+    def t_to(step):
+        return lax.rem(tensor + step, n_tensor)
+
+    def t_from(step):
+        return lax.rem(tensor + n_tensor - step, n_tensor)
+
+    def rows_of(index):
+        return pl.ds(pl.multiple_of(index * tok, tok), tok)
+
+    def teach_copy(rel, head, step, row_owner):
+        column = pl.multiple_of((to(step) * 2 + head) * tdh, tdh)
+        src = teachers[rel].at[:, pl.ds(column, tdh)]
+        dst = teach.at[rel, rows_of(row_owner), pl.ds(head * tdh, tdh)]
+        if step == 0:
+            return pltpu.make_async_copy(src, dst, teach_local.at[rel, head])
+        return pltpu.make_async_remote_copy(
+            src_ref=src, dst_ref=dst,
+            send_sem=teach_send.at[rel, head, step - 1], recv_sem=teach_recv.at[rel, head, step - 1],
+            device_id={"seq": base + to(step)}, device_id_type=pl.DeviceIdType.MESH,
+        )
+
+    def stud_copy(rel, step, row_owner):
+        column = pl.multiple_of((tensor * group_size + to(step)) * pair, pair)
+        src = students[rel].at[:, pl.ds(column, pair)]
+        dst = stud.at[rel, rows_of(row_owner), :]
+        if step == 0:
+            return pltpu.make_async_copy(src, dst, stud_local.at[rel])
+        return pltpu.make_async_remote_copy(
+            src_ref=src, dst_ref=dst,
+            send_sem=stud_send.at[rel, step - 1], recv_sem=stud_recv.at[rel, step - 1],
+            device_id={"seq": base + to(step)}, device_id_type=pl.DeviceIdType.MESH,
+        )
+
+    def out_copy(rel, step, owner):
+        src = result.at[rel, rows_of(to(step)), :]
+        column = pl.multiple_of((tensor * group_size + owner) * pair, pair)
+        dst = outs[rel].at[:, pl.ds(column, pair)]
+        if step == 0:
+            return pltpu.make_async_copy(src, dst, out_local.at[rel])
+        return pltpu.make_async_remote_copy(
+            src_ref=src, dst_ref=dst,
+            send_sem=out_send.at[rel, step - 1], recv_sem=out_recv.at[rel, step - 1],
+            device_id={"seq": base + to(step)}, device_id_type=pl.DeviceIdType.MESH,
+        )
+
+    def fwd_copy(rel, step, owner):
+        width = group_size * pair
+        columns = pl.ds(pl.multiple_of(owner * width, width), width)
+        return pltpu.make_async_remote_copy(
+            src_ref=outs[rel].at[:, columns], dst_ref=outs[rel].at[:, columns],
+            send_sem=fwd_send.at[rel, step - 1], recv_sem=fwd_recv.at[rel, step - 1],
+            device_id={"tensor": t_to(step)}, device_id_type=pl.DeviceIdType.MESH,
+        )
+
+    steps = range(1, group_size)
+    t_steps = range(1, n_tensor)
+    barrier = pltpu.get_barrier_semaphore()
+    for step in steps:
+        pl.semaphore_signal(
+            barrier, inc=1, device_id={"seq": base + to(step)}, device_id_type=pl.DeviceIdType.MESH
+        )
+    for step in t_steps:
+        pl.semaphore_signal(
+            barrier, inc=1, device_id={"tensor": t_to(step)}, device_id_type=pl.DeviceIdType.MESH
+        )
+
+    stud_copy(0, 0, member).start()
+    teach_copy(0, 0, 0, member).start()
+    pl.semaphore_wait(barrier, group_size - 1 + n_tensor - 1)
+
+    def start_stud(rel):
+        for step in steps:
+            stud_copy(rel, step, member).start()
+
+    def start_teach(rel, head):
+        for step in steps:
+            teach_copy(rel, head, step, member).start()
+
+    def finish_stud(rel):
+        stud_copy(rel, 0, member).wait()
+        for step in steps:
+            stud_copy(rel, step, source(step)).wait_recv()
+
+    def finish_teach(rel, head):
+        teach_copy(rel, head, 0, member).wait()
+        for step in steps:
+            teach_copy(rel, head, step, source(step)).wait_recv()
+
+    def start_out(rel):
+        out_copy(rel, 0, member).start()
+        for step in steps:
+            out_copy(rel, step, member).start()
+
+    def forward(rel):
+        out_copy(rel, 0, member).wait()
+        for step in steps:
+            out_copy(rel, step, source(step)).wait_recv()
+        for step in t_steps:
+            fwd_copy(rel, step, tensor).start()
+
+    start_stud(0)
+    start_teach(0, 0)
+    start_teach(0, 1)
+    for rel, head in ((0, 1), (1, 0), (1, 1)):
+        teach_copy(rel, head, 0, member).start()
+    stud_copy(1, 0, member).start()
+
+    for rel in range(2):
+        finish_stud(rel)
+        finish_teach(rel, 0)
+        if rel == 0:
+            start_stud(1)
+            start_teach(1, 0)
+        stud_t[...] = stud[rel].T
+        grad[...] = jnp.zeros_like(grad)
+        args = (teach.at[rel], stud.at[rel], stud_t, grad)
+        if rel == 1:
+            head_pass(*args, 0, 0, FORWARD_AFTER, tdh, sdh)
+            forward(0)
+            head_pass(*args, 0, FORWARD_AFTER, blocks, tdh, sdh)
+        else:
+            head_pass(*args, 0, 0, blocks, tdh, sdh)
+        finish_teach(rel, 1)
+        if rel == 0:
+            start_teach(1, 1)
+        head_pass(*args, 1, 0, blocks, tdh, sdh)
+        result[rel] = grad[...].astype(result.dtype)
+        start_out(rel)
+    forward(1)
+
+    for rel in range(2):
+        for step in t_steps:
+            fwd_copy(rel, step, t_from(step)).wait_recv()
+        for step in steps:
+            stud_copy(rel, step, member).wait_send()
+            teach_copy(rel, 0, step, member).wait_send()
+            teach_copy(rel, 1, step, member).wait_send()
+            out_copy(rel, step, member).wait_send()
+        for step in t_steps:
+            fwd_copy(rel, step, tensor).wait_send()
+
+
+def shards_pairs(teacher_q, teacher_v, student_q, student_v):
+    n_tensor = lax.axis_size("tensor")
+    group_size = lax.axis_size("seq") // SEQS
+    tdh = teacher_q.shape[1] * n_tensor // HEADS
+    sdh = student_q.shape[1] // HEADS
+    length = teacher_q.shape[0] * group_size
+    pair = 2 * sdh
+    dma = pltpu.SemaphoreType.DMA
+    out = jax.ShapeDtypeStruct(student_q.shape, student_q.dtype)
+    return pl.pallas_call(
+        functools.partial(fused_kernel, n_tensor, group_size, tdh, sdh),
+        out_shape=(out, out),
+        in_specs=[pl.BlockSpec(memory_space=pl.ANY)] * 4,
+        out_specs=(pl.BlockSpec(memory_space=pl.ANY),) * 2,
+        scratch_shapes=[
+            pltpu.VMEM((2, length, 2 * tdh), jnp.bfloat16),
+            pltpu.VMEM((2, length, pair), jnp.bfloat16),
+            pltpu.VMEM((pair, length), jnp.bfloat16),
+            pltpu.VMEM((length, pair), jnp.float32),
+            pltpu.VMEM((2, length, pair), jnp.bfloat16),
+            dma((2, 2, group_size - 1)),
+            dma((2, 2, group_size - 1)),
+            dma((2, 2)),
+            dma((2, group_size - 1)),
+            dma((2, group_size - 1)),
+            dma((2,)),
+            dma((2, group_size - 1)),
+            dma((2, group_size - 1)),
+            dma((2,)),
+            dma((2, n_tensor - 1)),
+            dma((2, n_tensor - 1)),
+        ],
+        compiler_params=pltpu.CompilerParams(
+            collective_id=0, has_side_effects=True, vmem_limit_bytes=56 * 2**20
+        ),
+    )(teacher_q, teacher_v, student_q, student_v)
 
 
 def from_partner(array, axis, distance):
@@ -94,6 +339,9 @@
 
 
 def solution(mesh):
+    per_dev = HEADS // mesh.shape["tensor"]
+    group_size = mesh.shape["seq"] // SEQS
+    body = shards_pairs if per_dev == 2 * group_size else shards
     in_specs = (P("seq", "tensor"), P("seq", "tensor"), P("seq", None), P("seq", None))
     out_specs = (P("seq", None), P("seq", None))
-    return jax.shard_map(shards, mesh=mesh, in_specs=in_specs, out_specs=out_specs, check_vma=False)
+    return jax.shard_map(body, mesh=mesh, in_specs=in_specs, out_specs=out_specs, check_vma=False)

time: 558 us -> 164 us (0.29)
  the two profiles are of different devices: /device:TPU:0 before, /device:TPU:11 now
where the time goes in v2:
time: 164 us
  Pallas kernels  159 us (97%)
  local copies, waits for them, and re-layouts  4.63 us (3%)
    pallas_call x1, Pallas kernels, shards_pairs(): pl.pallas_call(functools.partial(fused_kernel, n_tensor, group_size, tdh,...  159 us
    unnamed x4, local copies, waits for them, and re-layouts  4.63 us

profile of v2, /device:TPU:11, one launch (start us, length us, event | category | flops | bytes accessed | tf_op | source)
XLA Modules:
  0.0 164.0 jit_solution(15678904667272806692)
XLA Ops:
  0.6 158.7 %shard_map.59 = (bf16[512,2048]{1,0:T(8,128)(2,1)}, bf16[512,2048]{1,0:T(8,128)(2,1)}) custom-call(bf16[512,2048]{1,0:T(8,128)(2,1)} %teacher_q.1, bf16[512,2048]{1,0:T(8,128)(2,1)} %teacher_v.1, bf16[512,2048]{1,0:T(8,128)(2,1)} %student_q.1, bf16[512,2048]{1,0:T(8,128)(2,1)} %student_v.1), custom_call_target="tpu_custom_call" | custom-call | tf_op jit(solution)/shard_map/pallas_call | solution.py:226
  159.4 0.0 copy-start
  159.4 3.3 %copy.8 = bf16[512,2048]{1,0:T(8,128)(2,1)} copy(bf16[512,2048]{1,0:T(8,128)(2,1)} %get-tuple-element.4) | data formatting | bytes 4194304
  162.7 0.0 copy-done
  162.7 1.3 copy.9
Async XLA Ops:
  159.4 3.3 %copy-start = (bf16[512,2048]{1,0:T(8,128)(2,1)S(1)}, bf16[512,2048]{1,0:T(8,128)(2,1)}, u32[]{:S(2)}) copy-start(bf16[512,2048]{1,0:T(8,128)(2,1)} %get-tuple-element.5) | copy-start | bytes 6291460

commit v3 on v2

--- a/solution.py
+++ b/solution.py
@@ -11,48 +11,86 @@
 HEADS = 32
 SEQS = 2
 BLOCK = 256
-FORWARD_AFTER = 2
+CHUNK = 128
+PRODUCT = 256
+RELAYS = (((2, 0), (6, 1)), ((3, 2),))
 LOG2E = math.log2(math.e)
 
 
-def softmax_terms(scores, scale):
-    scaled = scores * (scale * LOG2E)
-    shifted = jnp.exp2(scaled - jnp.max(scaled, axis=0, keepdims=True))
-    return shifted, jnp.sum(shifted, axis=0, keepdims=True)
-
-
-def head_block(teach, stud, stud_t, grad, head, start, tdh, sdh):
-    rows = pl.ds(start, BLOCK)
+def prepare_head(stud, stud_t, masked, head, sdh):
+    lane = lax.broadcasted_iota(jnp.int32, stud.shape, 1)
+    masked[...] = jnp.where(lane // sdh == head, stud[...], jnp.zeros(stud.shape, stud.dtype))
+    stud_t[...] = masked[...].T
+
+
+def add_chunk(k, scores, scale, exps, tops, top, total):
+    size = scores.shape[0]
+    scores = scores.reshape(size // 8, 8, BLOCK) * (scale * LOG2E)
+    new_top = jnp.max(scores, axis=0)
+    if k:
+        new_top = jnp.maximum(top, new_top)
+    shifted = jnp.exp2(scores - new_top[None])
+    part = jnp.sum(shifted, axis=0)
+    new_total = total * jnp.exp2(top - new_top) + part if k else part
+    exps[k * size : (k + 1) * size, :] = shifted.reshape(size, BLOCK)
+    tops[k * 8 : (k + 1) * 8, :] = new_top
+    return new_top, new_total
+
+
+def finish_softmax(top, total, factor):
+    all_top = jnp.max(top, axis=0, keepdims=True)
+    return all_top, factor / jnp.sum(total * jnp.exp2(top - all_top), axis=0, keepdims=True)
+
+
+def head_pass(refs, head, first, last, tdh, sdh):
+    teach, stud, stud_t, masked, grad, teach_exps, stud_exps, teach_tops, stud_tops = refs
+    dims = (((1,), (1,)), ((), ()))
+    length = stud.shape[0]
     columns = slice(head * tdh, (head + 1) * tdh)
-    dims = (((1,), (1,)), ((), ()))
-    stud_own = stud[rows, :]
-    lane = lax.broadcasted_iota(jnp.int32, stud_own.shape, 1)
-    masked = jnp.where(lane // sdh == head, stud_own, jnp.zeros_like(stud_own))
-    teach_scores = lax.dot_general(
-        teach[:, columns], teach[rows, columns], dims, preferred_element_type=jnp.float32
-    )
-    stud_scores = lax.dot_general(stud[...], masked, dims, preferred_element_type=jnp.float32)
-    teach_exp, teach_sum = softmax_terms(teach_scores, tdh**-0.5)
-    stud_exp, stud_sum = softmax_terms(stud_scores, sdh**-0.5)
     factor = 256.0 * sdh**-0.5
-    coef = (stud_exp * (factor / stud_sum) - teach_exp * (factor / teach_sum)).astype(jnp.bfloat16)
-    grad[...] += jnp.dot(coef, masked, preferred_element_type=jnp.float32)
-    query_side = jnp.dot(stud_t[...], coef, preferred_element_type=jnp.float32)
-    sub = lax.broadcasted_iota(jnp.int32, query_side.shape, 0)
-    query_side = jnp.where(sub // sdh == head, query_side, 0.0)
-    grad[rows, :] += query_side.T
-
-
-def head_pass(teach, stud, stud_t, grad, head, first, last, tdh, sdh):
+
     @pl.loop(first, last)
     def _(block):
-        head_block(teach, stud, stud_t, grad, head, pl.multiple_of(block * BLOCK, BLOCK), tdh, sdh)
+        rows = pl.ds(pl.multiple_of(block * BLOCK, BLOCK), BLOCK)
+        teach_own = teach[rows, columns]
+        stud_own = masked[rows, :]
+        t_top = t_total = s_top = s_total = None
+        for k in range(length // CHUNK):
+            keys = slice(k * CHUNK, (k + 1) * CHUNK)
+            teach_scores = lax.dot_general(
+                teach[keys, columns], teach_own, dims, preferred_element_type=jnp.float32
+            )
+            stud_scores = lax.dot_general(
+                stud[keys, :], stud_own, dims, preferred_element_type=jnp.float32
+            )
+            t_top, t_total = add_chunk(k, teach_scores, tdh**-0.5, teach_exps, teach_tops, t_top, t_total)
+            s_top, s_total = add_chunk(k, stud_scores, sdh**-0.5, stud_exps, stud_tops, s_top, s_total)
+        t_top, t_factor = finish_softmax(t_top, t_total, factor)
+        s_top, s_factor = finish_softmax(s_top, s_total, factor)
+        query_side = None
+        for k in range(length // PRODUCT):
+            parts = []
+            for c in range(k * PRODUCT // CHUNK, (k + 1) * PRODUCT // CHUNK):
+                keys, top_rows = slice(c * CHUNK, (c + 1) * CHUNK), slice(c * 8, (c + 1) * 8)
+                t_mul = jnp.exp2(teach_tops[top_rows, :] - t_top) * t_factor
+                s_mul = jnp.exp2(stud_tops[top_rows, :] - s_top) * s_factor
+                coef = (
+                    stud_exps[keys, :].reshape(CHUNK // 8, 8, BLOCK) * s_mul[None]
+                    - teach_exps[keys, :].reshape(CHUNK // 8, 8, BLOCK) * t_mul[None]
+                )
+                parts.append(coef.reshape(CHUNK, BLOCK).astype(jnp.bfloat16))
+            coef = jnp.concatenate(parts, axis=0)
+            keys = slice(k * PRODUCT, (k + 1) * PRODUCT)
+            grad[keys, :] += jnp.dot(coef, stud_own, preferred_element_type=jnp.float32)
+            part = jnp.dot(stud_t[:, keys], coef, preferred_element_type=jnp.float32)
+            query_side = part if query_side is None else query_side + part
+        grad[rows, :] += query_side.T
 
 
 def fused_kernel(
     n_tensor, group_size, tdh, sdh,
     teacher_q, teacher_v, student_q, student_v, out_q, out_v,
-    teach, stud, stud_t, grad, result,
+    teach, stud, stud_t, masked, grad, teach_exps, stud_exps, teach_tops, stud_tops, result,
     teach_send, teach_recv, teach_local, stud_send, stud_recv, stud_local,
     out_send, out_recv, out_local, fwd_send, fwd_recv,
 ):
@@ -72,12 +110,6 @@
     def source(step):
         return lax.rem(member + group_size - step, group_size)
 
-    def t_to(step):
-        return lax.rem(tensor + step, n_tensor)
-
-    def t_from(step):
-        return lax.rem(tensor + n_tensor - step, n_tensor)
-
     def rows_of(index):
         return pl.ds(pl.multiple_of(index * tok, tok), tok)
 
@@ -117,25 +149,70 @@
             device_id={"seq": base + to(step)}, device_id_type=pl.DeviceIdType.MESH,
         )
 
-    def fwd_copy(rel, step, owner):
-        width = group_size * pair
-        columns = pl.ds(pl.multiple_of(owner * width, width), width)
+    def relay_copy(rel, step, way, chunk):
+        origin = tensor - step if way == 0 else tensor + step
+        column = pl.multiple_of((origin * group_size + source(chunk)) * pair, pair)
+        block = outs[rel].at[:, pl.ds(column, pair)]
         return pltpu.make_async_remote_copy(
-            src_ref=outs[rel].at[:, columns], dst_ref=outs[rel].at[:, columns],
-            send_sem=fwd_send.at[rel, step - 1], recv_sem=fwd_recv.at[rel, step - 1],
-            device_id={"tensor": t_to(step)}, device_id_type=pl.DeviceIdType.MESH,
-        )
+            src_ref=block, dst_ref=block,
+            send_sem=fwd_send.at[rel, way, step, chunk], recv_sem=fwd_recv.at[rel, way, step, chunk],
+            device_id={"tensor": tensor + 1 if way == 0 else tensor - 1},
+            device_id_type=pl.DeviceIdType.MESH,
+        )
+
+    def has_origin(step, way):
+        return tensor >= step if way == 0 else tensor + step < n_tensor
+
+    def has_next(way):
+        return tensor + 1 < n_tensor if way == 0 else tensor > 0
+
+    def arrived(rel, step, way, chunk):
+        origin = tensor - step if way == 0 else tensor + step
+        column = pl.multiple_of((origin * group_size + source(chunk)) * pair, pair)
+        block = outs[rel].at[:, pl.ds(column, pair)]
+        pltpu.make_async_remote_copy(
+            src_ref=block, dst_ref=block,
+            send_sem=fwd_send.at[rel, way, step - 1, chunk], recv_sem=fwd_recv.at[rel, way, step - 1, chunk],
+            device_id={"tensor": tensor + 1 if way == 0 else tensor - 1},
+            device_id_type=pl.DeviceIdType.MESH,
+        ).wait_recv()
+
+    def relay(rel, step):
+        for chunk in range(group_size):
+            if step == 0:
+                if chunk == 0:
+                    out_copy(rel, 0, member).wait()
+                else:
+                    out_copy(rel, chunk, source(chunk)).wait_recv()
+            for way in range(2):
+                if step:
+                    @pl.when(has_origin(step, way))
+                    def _():
+                        arrived(rel, step, way, chunk)
+
+                if step < n_tensor - 1:
+                    @pl.when(has_origin(step, way) & has_next(way))
+                    def _():
+                        relay_copy(rel, step, way, chunk).start()
+
+    def relay_sent(rel):
+        for step in range(n_tensor - 1):
+            for way in range(2):
+                @pl.when(has_origin(step, way) & has_next(way))
+                def _():
+                    for chunk in range(group_size):
+                        relay_copy(rel, step, way, chunk).wait_send()
 
     steps = range(1, group_size)
-    t_steps = range(1, n_tensor)
     barrier = pltpu.get_barrier_semaphore()
     for step in steps:
         pl.semaphore_signal(
             barrier, inc=1, device_id={"seq": base + to(step)}, device_id_type=pl.DeviceIdType.MESH
         )
-    for step in t_steps:
+    for step in range(1, n_tensor):
         pl.semaphore_signal(
-            barrier, inc=1, device_id={"tensor": t_to(step)}, device_id_type=pl.DeviceIdType.MESH
+            barrier, inc=1, device_id={"tensor": lax.rem(tensor + step, n_tensor)},
+            device_id_type=pl.DeviceIdType.MESH,
         )
 
     stud_copy(0, 0, member).start()
@@ -164,13 +241,6 @@
         out_copy(rel, 0, member).start()
         for step in steps:
             out_copy(rel, step, member).start()
-
-    def forward(rel):
-        out_copy(rel, 0, member).wait()
-        for step in steps:
-            out_copy(rel, step, source(step)).wait_recv()
-        for step in t_steps:
-            fwd_copy(rel, step, tensor).start()
 
     start_stud(0)
     start_teach(0, 0)
@@ -185,33 +255,37 @@
         if rel == 0:
             start_stud(1)
             start_teach(1, 0)
-        stud_t[...] = stud[rel].T
         grad[...] = jnp.zeros_like(grad)
-        args = (teach.at[rel], stud.at[rel], stud_t, grad)
-        if rel == 1:
-            head_pass(*args, 0, 0, FORWARD_AFTER, tdh, sdh)
-            forward(0)
-            head_pass(*args, 0, FORWARD_AFTER, blocks, tdh, sdh)
-        else:
-            head_pass(*args, 0, 0, blocks, tdh, sdh)
-        finish_teach(rel, 1)
-        if rel == 0:
-            start_teach(1, 1)
-        head_pass(*args, 1, 0, blocks, tdh, sdh)
+        refs = (
+            teach.at[rel], stud.at[rel], stud_t, masked, grad,
+            teach_exps, stud_exps, teach_tops, stud_tops,
+        )
+        for head in range(2):
+            if head:
+                finish_teach(rel, 1)
+                if rel == 0:
+                    start_teach(1, 1)
+            prepare_head(*refs[1:4], head, sdh)
+            first = 0
+            if rel:
+                for at, step in RELAYS[head]:
+                    head_pass(refs, head, first, blocks * at // 8, tdh, sdh)
+                    relay(0, step)
+                    first = blocks * at // 8
+            head_pass(refs, head, first, blocks, tdh, sdh)
         result[rel] = grad[...].astype(result.dtype)
         start_out(rel)
-    forward(1)
+    relay(0, n_tensor - 1)
+    for step in range(n_tensor):
+        relay(1, step)
 
     for rel in range(2):
-        for step in t_steps:
-            fwd_copy(rel, step, t_from(step)).wait_recv()
         for step in steps:
             stud_copy(rel, step, member).wait_send()
             teach_copy(rel, 0, step, member).wait_send()
             teach_copy(rel, 1, step, member).wait_send()
             out_copy(rel, step, member).wait_send()
-        for step in t_steps:
-            fwd_copy(rel, step, tensor).wait_send()
+        relay_sent(rel)
 
 
 def shards_pairs(teacher_q, teacher_v, student_q, student_v):
@@ -232,7 +306,12 @@
             pltpu.VMEM((2, length, 2 * tdh), jnp.bfloat16),
             pltpu.VMEM((2, length, pair), jnp.bfloat16),
             pltpu.VMEM((pair, length), jnp.bfloat16),
+            pltpu.VMEM((length, pair), jnp.bfloat16),
             pltpu.VMEM((length, pair), jnp.float32),
+            pltpu.VMEM((length, BLOCK), jnp.float32),
+            pltpu.VMEM((length, BLOCK), jnp.float32),
+            pltpu.VMEM((length // CHUNK * 8, BLOCK), jnp.float32),
+            pltpu.VMEM((length // CHUNK * 8, BLOCK), jnp.float32),
             pltpu.VMEM((2, length, pair), jnp.bfloat16),
             dma((2, 2, group_size - 1)),
             dma((2, 2, group_size - 1)),
@@ -243,8 +322,8 @@
             dma((2, group_size - 1)),
             dma((2, group_size - 1)),
             dma((2,)),
-            dma((2, n_tensor - 1)),
-            dma((2, n_tensor - 1)),
+            dma((2, 2, n_tensor - 1, group_size)),
+            dma((2, 2, n_tensor - 1, group_size)),
         ],
         compiler_params=pltpu.CompilerParams(
             collective_id=0, has_side_effects=True, vmem_limit_bytes=56 * 2**20
@@ -341,7 +420,7 @@
 def solution(mesh):
     per_dev = HEADS // mesh.shape["tensor"]
     group_size = mesh.shape["seq"] // SEQS
-    body = shards_pairs if per_dev == 2 * group_size else shards
+    body = shards_pairs if per_dev == 2 * group_size and mesh.shape["tensor"] == 4 else shards
     in_specs = (P("seq", "tensor"), P("seq", "tensor"), P("seq", None), P("seq", None))
     out_specs = (P("seq", None), P("seq", None))
     return jax.shard_map(body, mesh=mesh, in_specs=in_specs, out_specs=out_specs, check_vma=False)

time: 164 us -> 140 us (0.85)
  the two profiles are of different devices: /device:TPU:11 before, /device:TPU:0 now
where the time goes in v3:
time: 140 us
  Pallas kernels  135 us (96%)
  local copies, waits for them, and re-layouts  4.63 us (3%)
    pallas_call x1, Pallas kernels, shards_pairs(): pl.pallas_call(functools.partial(fused_kernel, n_tensor, group_size, tdh,...  135 us
    unnamed x4, local copies, waits for them, and re-layouts  4.63 us

profile of v3, /device:TPU:0, one launch (start us, length us, event | category | flops | bytes accessed | tf_op | source)
XLA Modules:
  0.0 140.0 jit_solution(6636502157634917294)
XLA Ops:
  0.6 134.8 %shard_map.59 = (bf16[512,2048]{1,0:T(8,128)(2,1)}, bf16[512,2048]{1,0:T(8,128)(2,1)}) custom-call(bf16[512,2048]{1,0:T(8,128)(2,1)} %teacher_q.1, bf16[512,2048]{1,0:T(8,128)(2,1)} %teacher_v.1, bf16[512,2048]{1,0:T(8,128)(2,1)} %student_q.1, bf16[512,2048]{1,0:T(8,128)(2,1)} %student_v.1), custom_call_target="tpu_custom_call" | custom-call | tf_op jit(solution)/shard_map/pallas_call | solution.py:300
  135.4 0.0 copy-start
  135.4 3.3 %copy.8 = bf16[512,2048]{1,0:T(8,128)(2,1)} copy(bf16[512,2048]{1,0:T(8,128)(2,1)} %get-tuple-element.4) | data formatting | bytes 4194304
  138.7 0.0 copy-done
  138.7 1.3 copy.9
Async XLA Ops:
  135.4 3.3 %copy-start = (bf16[512,2048]{1,0:T(8,128)(2,1)S(1)}, bf16[512,2048]{1,0:T(8,128)(2,1)}, u32[]{:S(2)}) copy-start(bf16[512,2048]{1,0:T(8,128)(2,1)} %get-tuple-element.5) | copy-start | bytes 6291460
